TPU v7x, 256 devices: a whole 4x4x8 slice. The times are simulated.
256 devices in a mesh: gx: 8 (over y, x_lo), gy: 2 (over x_hi), vert: 16 (over z, core).
Axes of the slice: x: 4 (x_hi: 2, x_lo: 2; x = x_hi * 2 + x_lo), y: 4, z: 8, core: 2. Of those that a mesh axis runs over, the one named last changes fastest.
Arguments:
- state: float32 [8000, 3, 4, 1024], P('vert', None, 'gy', 'gx'), as said below
- tangent: float32 [8000, 3, 4, 1024], P('vert', None, 'gy', 'gx')
- orient: int32 [8000, 2], P('vert'), may hold values from 0 to 1, as said below
- walls: int32 [2, 1024], P(None, 'gx'), may hold values from 0 to 1
Outputs:
- product: float32 [8000, 3, 4, 1024], P('vert', None, 'gy', 'gx')
Inputs may be any that keep to these rules, and one draw needn't show every extreme that they name: In every aligned group of four slots 4k to 4k+3 there are two bits p, r with orient[4k + 2b + e] = (e XOR p, b XOR r) for b, e in 0, 1. The state's values at the four points q of every cell are positive.
All inputs are finite; a program needn't handle non-finite values.
Results may differ from a plain program's by a relative error of at most 0.0003.
Values sent between devices are 32-bit elements; how exact they have to be, the bound alone decides.
A program may use at most 64 MiB of HBM per device.

v0:
```python
import math
import jax
import jax.numpy as jnp
from jax import lax
from jax.sharding import PartitionSpec as P

NVX = 20
GAUSS = 0.5773502691896258
XI_SIGNS = (-1.0, -1.0, 1.0, 1.0)
ETA_SIGNS = (-1.0, 1.0, -1.0, 1.0)
MIRRORED_DUOS = ((0, 0), (1, 1), (2, 2), (0, 1), (0, 2), (1, 2))
COLLIDE = 2.0
LOG_TWO_PI = math.log(2.0 * math.pi)


def padded(block, sides, width, periodic):
    for axis, dim in sides:
        count = lax.axis_size(axis)
        forward = [(i, i + 1) for i in range(count - 1)]
        if periodic:
            forward.append((count - 1, 0))
        backward = [(target, source) for source, target in forward]
        low = lax.ppermute(
            lax.slice_in_dim(block, block.shape[dim] - width, None, axis=dim), axis, forward
        )
        high = lax.ppermute(lax.slice_in_dim(block, 0, width, axis=dim), axis, backward)
        block = jnp.concatenate([low, block, high], axis=dim)
    return block


def velocities(slot_index, orient, half_grid):
    spacing = 5.0 / half_grid
    mag_x = (slot_index // (4 * half_grid) % half_grid).astype(jnp.float32) + 0.5
    mag_y = (slot_index // 4 % half_grid).astype(jnp.float32) + 0.5
    level_z = (slot_index // (4 * half_grid * half_grid)).astype(jnp.float32) - (half_grid - 0.5)
    sign_x = (2 * orient[:, 0] - 1).astype(jnp.float32)
    sign_y = (2 * orient[:, 1] - 1).astype(jnp.float32)
    return (sign_x * mag_x * spacing, sign_y * mag_y * spacing, level_z * spacing)


def moment_table(vel_x, vel_y, molecular_grid_extent, weight):
    return (
        jnp.stack(
            [
                jnp.ones_like(vel_x),
                vel_x,
                vel_y,
                molecular_grid_extent,
                vel_x * vel_x,
                vel_y * vel_y,
                molecular_grid_extent * molecular_grid_extent,
                vel_x * vel_y,
                vel_x * molecular_grid_extent,
                vel_y * molecular_grid_extent,
            ]
        )
        * weight
    )


def gauss_points(coef):
    center, grad_x, grad_y = (coef[:, 0], coef[:, 1], coef[:, 2])
    return jnp.stack(
        [center + XI_SIGNS[q] * GAUSS * grad_x + ETA_SIGNS[q] * GAUSS * grad_y for q in range(4)],
        axis=1,
    )


def project_points(values):
    total = values[:, 0] + values[:, 1] + values[:, 2] + values[:, 3]
    along_x = values[:, 2] + values[:, 3] - (values[:, 0] + values[:, 1])
    along_y = values[:, 1] + values[:, 3] - (values[:, 0] + values[:, 2])
    return jnp.stack([0.25 * total, 0.75 * GAUSS * along_x, 0.75 * GAUSS * along_y], axis=1)


def partner(values):
    dims_in = values.shape
    grouped = values.reshape((dims_in[0] // 4, 2, 2) + dims_in[1:])
    return grouped[:, ::-1].reshape(dims_in)


def full_matrix(entries):
    rows = [[None, None, None], [None, None, None], [None, None, None]]
    for duo_ordinal, (leading_multiplier, trailing_multiplier) in enumerate(MIRRORED_DUOS):
        rows[leading_multiplier][trailing_multiplier] = entries[duo_ordinal]
        rows[trailing_multiplier][leading_multiplier] = entries[duo_ordinal]
    return rows


def gauss_params(moments):
    density = moments[0]
    average_offset = [moments[1 + leading_multiplier] / density for leading_multiplier in range(3)]
    second = [moments[4 + duo_ordinal] for duo_ordinal in range(6)]
    covariance_array = [
        second[duo_ordinal] / density
        - average_offset[leading_multiplier] * average_offset[trailing_multiplier]
        for duo_ordinal, (leading_multiplier, trailing_multiplier) in enumerate(MIRRORED_DUOS)
    ]
    thermal_state = (covariance_array[0] + covariance_array[1] + covariance_array[2]) / 3.0
    pressure_dyad = [
        (1.5 * thermal_state if leading_multiplier == trailing_multiplier else 0.0)
        - 0.5 * covariance_array[duo_ordinal]
        for duo_ordinal, (leading_multiplier, trailing_multiplier) in enumerate(MIRRORED_DUOS)
    ]
    tens_full = full_matrix(pressure_dyad)
    cofactor = [
        tens_full[1][1] * tens_full[2][2] - tens_full[1][2] * tens_full[1][2],
        tens_full[0][0] * tens_full[2][2] - tens_full[0][2] * tens_full[0][2],
        tens_full[0][0] * tens_full[1][1] - tens_full[0][1] * tens_full[0][1],
        tens_full[0][2] * tens_full[1][2] - tens_full[0][1] * tens_full[2][2],
        tens_full[0][1] * tens_full[1][2] - tens_full[0][2] * tens_full[1][1],
        tens_full[0][1] * tens_full[0][2] - tens_full[0][0] * tens_full[1][2],
    ]
    determinant = (
        tens_full[0][0] * cofactor[0]
        + tens_full[0][1] * cofactor[3]
        + tens_full[0][2] * cofactor[4]
    )
    inverse = [entry / determinant for entry in cofactor]
    log_pre = jnp.log(density) - 1.5 * LOG_TWO_PI - 0.5 * jnp.log(determinant)
    delta_density = moments[10]
    drift_delta = [
        (moments[11 + leading_multiplier] - average_offset[leading_multiplier] * delta_density)
        / density
        for leading_multiplier in range(3)
    ]
    dtheta = [
        moments[14 + duo_ordinal] / density
        - second[duo_ordinal] * delta_density / (density * density)
        - (
            drift_delta[leading_multiplier] * average_offset[trailing_multiplier]
            + average_offset[leading_multiplier] * drift_delta[trailing_multiplier]
        )
        for duo_ordinal, (leading_multiplier, trailing_multiplier) in enumerate(MIRRORED_DUOS)
    ]
    temp_delta = (dtheta[0] + dtheta[1] + dtheta[2]) / 3.0
    tens_delta = [
        (1.5 * temp_delta if leading_multiplier == trailing_multiplier else 0.0)
        - 0.5 * dtheta[duo_ordinal]
        for duo_ordinal, (leading_multiplier, trailing_multiplier) in enumerate(MIRRORED_DUOS)
    ]
    inv_full = full_matrix(inverse)
    delta_full = full_matrix(tens_delta)
    trace_term = sum(
        [
            inv_full[leading_multiplier][trailing_multiplier]
            * delta_full[trailing_multiplier][leading_multiplier]
            for leading_multiplier in range(3)
            for trailing_multiplier in range(3)
        ]
    )
    shift_term = delta_density / density - 0.5 * trace_term
    weight_vec = [
        inv_full[leading_multiplier][0] * drift_delta[0]
        + inv_full[leading_multiplier][1] * drift_delta[1]
        + inv_full[leading_multiplier][2] * drift_delta[2]
        for leading_multiplier in range(3)
    ]
    inner_prod = [
        [
            inv_full[leading_multiplier][0] * delta_full[0][c]
            + inv_full[leading_multiplier][1] * delta_full[1][c]
            + inv_full[leading_multiplier][2] * delta_full[2][c]
            for c in range(3)
        ]
        for leading_multiplier in range(3)
    ]
    curve_sym = [
        inner_prod[leading_multiplier][0] * inv_full[0][trailing_multiplier]
        + inner_prod[leading_multiplier][1] * inv_full[1][trailing_multiplier]
        + inner_prod[leading_multiplier][2] * inv_full[2][trailing_multiplier]
        for leading_multiplier, trailing_multiplier in MIRRORED_DUOS
    ]
    return jnp.stack(average_offset + inverse + [log_pre, shift_term] + weight_vec + curve_sym)


def quadratic(entries, rel_x, rel_y, rel_z):
    return (
        entries[0] * rel_x * rel_x
        + entries[1] * rel_y * rel_y
        + entries[2] * rel_z * rel_z
        + 2.0
        * (entries[3] * rel_x * rel_y + entries[4] * rel_x * rel_z + entries[5] * rel_y * rel_z)
    )


def gauss_tangent(vel_x, vel_y, molecular_grid_extent, params):
    rel_x = vel_x[:, None] - params[0]
    rel_y = vel_y[:, None] - params[1]
    rel_z = molecular_grid_extent[:, None] - params[2]
    gauss = jnp.exp(params[9] - 0.5 * quadratic(params[3:9], rel_x, rel_y, rel_z))
    return gauss * (
        params[10]
        + rel_x * params[11]
        + rel_y * params[12]
        + rel_z * params[13]
        + 0.5 * quadratic(params[14:20], rel_x, rel_y, rel_z)
    )


def transport(coef, orient, vel_x, vel_y, left_in, right_in, below_in, above_in):
    center, grad_x, grad_y = (coef[:, 0], coef[:, 1], coef[:, 2])
    heads_right = (orient[:, 0] == 1)[:, None, None]
    heads_up = (orient[:, 1] == 1)[:, None, None]
    right_val = jnp.where(heads_right, center + grad_x, right_in[0])
    right_slope = jnp.where(heads_right, grad_y, right_in[1])
    left_val = jnp.where(heads_right, left_in[0], center - grad_x)
    left_slope = jnp.where(heads_right, left_in[1], grad_y)
    top_val = jnp.where(heads_up, center + grad_y, above_in[0])
    top_slope = jnp.where(heads_up, grad_x, above_in[1])
    bottom_val = jnp.where(heads_up, below_in[0], center - grad_y)
    bottom_slope = jnp.where(heads_up, below_in[1], grad_x)
    speed_x = vel_x[:, None, None]
    speed_y = vel_y[:, None, None]
    rate_mean = speed_x * (right_val - left_val) + speed_y * (top_val - bottom_val)
    rate_x = 3.0 * speed_x * (right_val + left_val - 2.0 * center) + speed_y * (
        top_slope - bottom_slope
    )
    rate_y = speed_x * (right_slope - left_slope) + 3.0 * speed_y * (
        top_val + bottom_val - 2.0 * center
    )
    return jnp.stack([rate_mean, rate_x, rate_y], axis=1)


def shards(state, tangent, orient, walls):
    slots_here = state.shape[0]
    cell_rows = state.shape[2]
    cell_cols = state.shape[3]
    half_grid = NVX // 2
    weight = (5.0 / half_grid) ** 3
    point_count = 4 * cell_rows * cell_cols
    slot_index = lax.axis_index("vert") * slots_here + jnp.arange(slots_here, dtype=jnp.int32)
    vel_x, vel_y, molecular_grid_extent = velocities(slot_index, orient, half_grid)
    moment_rows = moment_table(vel_x, vel_y, molecular_grid_extent, weight)
    stacked = jnp.concatenate(
        [
            gauss_points(state).reshape(slots_here, point_count),
            gauss_points(tangent).reshape(slots_here, point_count),
        ],
        axis=1,
    )
    partial_sums = jnp.dot(
        moment_rows, stacked, precision=lax.Precision.HIGHEST, preferred_element_type=jnp.float32
    )
    partial_sums = jnp.concatenate(
        [partial_sums[:, :point_count], partial_sums[:, point_count:]], axis=0
    )
    params = gauss_params(lax.psum(partial_sums, "vert"))
    center, grad_x, grad_y = (tangent[:, 0], tangent[:, 1], tangent[:, 2])
    x_padded = padded(tangent, (("gx", 3),), 1, True)
    western = x_padded[:, :, :, :-2]
    eastern = x_padded[:, :, :, 2:]
    left_in = (western[:, 0] + western[:, 1], western[:, 2])
    right_in = (eastern[:, 0] - eastern[:, 1], eastern[:, 2])
    y_padded = padded(tangent, (("gy", 2),), 1, False)
    southern = y_padded[:, :, :-2]
    northern = y_padded[:, :, 2:]
    below_in = (southern[:, 0] + southern[:, 2], southern[:, 1])
    above_in = (northern[:, 0] - northern[:, 2], northern[:, 1])
    floor_flag = walls[0].astype(jnp.float32)
    roof_flag = walls[1].astype(jnp.float32)
    at_bottom = lax.axis_index("gy") == 0
    at_top = lax.axis_index("gy") == lax.axis_size("gy") - 1
    floor_val = (floor_flag * partner(center - grad_y)[:, 0], floor_flag * partner(grad_x)[:, 0])
    roof_val = (roof_flag * partner(center + grad_y)[:, -1], roof_flag * partner(grad_x)[:, -1])
    below_in = tuple(
        (
            jnp.concatenate(
                [jnp.where(at_bottom, wall_part, field_part[:, 0])[:, None], field_part[:, 1:]],
                axis=1,
            )
            for field_part, wall_part in zip(below_in, floor_val)
        )
    )
    above_in = tuple(
        (
            jnp.concatenate(
                [field_part[:, :-1], jnp.where(at_top, wall_part, field_part[:, -1])[:, None]],
                axis=1,
            )
            for field_part, wall_part in zip(above_in, roof_val)
        )
    )
    advected = transport(tangent, orient, vel_x, vel_y, left_in, right_in, below_in, above_in)
    gauss_delta = gauss_tangent(vel_x, vel_y, molecular_grid_extent, params).reshape(
        slots_here, 4, cell_rows, cell_cols
    )
    return advected + COLLIDE * (tangent - project_points(gauss_delta))


def solution(mesh):
    placed = (
        P("vert", None, "gy", "gx"),
        P("vert", None, "gy", "gx"),
        P("vert", None),
        P(None, "gx"),
    )
    return jax.shard_map(
        shards, mesh=mesh, in_specs=placed, out_specs=P("vert", None, "gy", "gx"), check_vma=False
    )
```

profile of v0, /device:TPU:1, one launch (start us, length us, event | category | flops | bytes accessed | tf_op | source)
XLA Modules:
  0.0 193.0 jit_solution(14825529700817234752)
XLA Ops:
  6.5 0.8 fusion.80
  7.5 2.6 %multiply_add_fusion.9 = (f32[500,1,2,128]{3,2,1,0:T(2,128)S(1)}, f32[500,1,2,128]{3,2,1,0:T(2,128)S(1)}, f32[500,1,2,128]{3,2,1,0:T(2,128)S(1)}, f32[500,1,2,12...) fusion(f32[500,3,2,128]{3,2,1,0:T(2,128)} %param.5), kind=kLoop, calls=%fused_computation.98 | loop fusion | flops 1536000 | bytes 5120000 | tf_op jit(solution)/shard_map/add | solution.py:64
  10.1 1.9 pad_maximum_fusion.1
  12.0 3.9 %reshape.660 = f32[500,1024]{1,0:T(8,128)} reshape(f32[500,4,2,128]{3,2,1,0:T(2,128)} %pad_maximum_fusion.1) | data formatting | bytes 4096000 | tf_op jit(solution)/shard_map/reshape | solution.py:238
  15.8 2.3 %multiply_add_fusion.13 = (f32[500,1,2,128]{3,2,1,0:T(2,128)S(1)}, f32[500,1,2,128]{3,2,1,0:T(2,128)S(1)}, f32[500,1,2,128]{3,2,1,0:T(2,128)S(1)}, f32[500,1,2,128]{3,2,1,0:T(2,128)S(1)}) fusion(f32[500,3,2,128]{3,2,1,0:T(2,128)} %param.4), kind=kLoop, calls=%fused_computation.102 | loop fusion | flops 1280000 | bytes 3584000 | tf_op jit(solution)/shard_map/add | solution.py:64
  18.1 1.9 pad_maximum_fusion
  20.0 3.9 %reshape.659 = f32[500,1024]{1,0:T(8,128)} reshape(f32[500,4,2,128]{3,2,1,0:T(2,128)} %pad_maximum_fusion) | data formatting | bytes 4096000 | tf_op jit(solution)/shard_map/reshape | solution.py:237
  23.9 0.1 stack.11
  24.0 4.4 %fusion = f32[10,2048]{1,0:T(8,128)S(1)} fusion(f32[500,1024]{1,0:T(8,128)} %reshape.660, f32[500,1024]{1,0:T(8,128)} %reshape.659, f32[10,500]{1,0:T(8,128)S(1)} %stack.11), kind=kOutput, calls=%fused_computation.27 | convolution fusion | flops 123909000 | bytes 4197920 | tf_op jit(solution)/shard_map/dot_general | solution.py:242
  28.4 0.7 pad_maximum_fusion.8
  29.1 0.0 all-reduce.2.cloned.1.call-update
  29.1 2.3 %fusion.102 = (f32[500,3,1,128]{3,2,0,1:T(1,128)}, f32[500,3,1,128]{3,2,0,1:T(1,128)}) fusion(f32[500,3,2,128]{3,2,1,0:T(2,128)S(1)} %copy-done), kind=kLoop, calls=%fused_computation.265 | loop fusion | bytes 3072000 | tf_op jit(solution)/shard_map/slice | solution.py:26
  31.4 1.3 collective-permute-start.2
  32.7 7.3 %collective-permute-start.3 = (f32[500,3,1,128]{3,2,0,1:T(1,128)}, f32[500,3,1,128]{3,2,0,1:T(1,128)}, u32[]{:S(2)}, u32[]{:S(2)}) collective-permute-start(f32[500,3,1,128]{3,2,0,1:T(1,128)} %get-tuple-element.79), channel_id=1, source_target_pairs={{0,16},{1,17},{2,18},{3,19},{4,20},{5,21},{6,22},{7,23},{8,24},{9,... | collective-permute-start | bytes 2304008 | tf_op jit(solution)/shard_map/ppermute | solution.py:23
  40.0 3.8 %fusion.103 = (f32[500,3,2,1]{3,2,1,0:T(2,128)}, f32[500,3,2,1]{3,2,1,0:T(2,128)}) fusion(f32[500,3,2,128]{3,2,1,0:T(2,128)S(1)} %copy-done), kind=kLoop, calls=%fused_computation.266 | loop fusion | bytes 48000 | tf_op jit(solution)/shard_map/slice | solution.py:26
  43.7 2.5 %copy.33 = f32[500,3,2,1]{0,2,3,1:T(2,128)S(1)} copy(f32[500,3,2,1]{3,2,1,0:T(2,128)} %get-tuple-element.80) | data formatting | bytes 24000
  46.2 4.5 %collective-permute-start = (f32[500,3,2,1]{0,2,3,1:T(2,128)S(1)}, f32[500,3,2,1]{0,2,3,1:T(2,128)S(1)}, u32[]{:S(2)}, u32[]{:S(2)}) collective-permute-start(f32[500,3,2,1]{0,2,3,1:T(2,128)S(1)} %copy.33), channel_id=1, source_target_pairs={{32,0},{64,32},{96,64},{128,96},{160,128},{192,160},{224,192},{0,2... | collective-permute-start | bytes 36008 | tf_op jit(solution)/shard_map/ppermute | solution.py:26
  50.7 2.4 %copy.34 = f32[500,3,2,1]{0,2,3,1:T(2,128)S(1)} copy(f32[500,3,2,1]{3,2,1,0:T(2,128)} %get-tuple-element.81) | data formatting | bytes 24000
  53.2 0.1 collective-permute-start.1
  53.4 0.0 copy-done.2
  53.4 1.0 rev.11
  54.4 1.0 rev.12
  55.4 1.0 rev.10
  56.4 1.6 collective-permute-done
  58.0 1.1 copy.18
  59.1 1.2 collective-permute-done.1
  60.3 2.0 %copy.20 = f32[500,3,2,1]{3,2,1,0:T(2,128)} copy(f32[500,3,2,1]{0,2,3,1:T(2,128)S(1)} %collective-permute-done.1) | data formatting | bytes 24000 | tf_op jit(solution)/shard_map/ppermute | solution.py:23
  62.3 77.0 %all-reduce.2.cloned.1.call-done = f32[20,1024]{1,0:T(8,128)} async-done(((f32[20,1024]{1,0:T(8,128)}), f32[20,1024]{1,0:T(8,128)}) %all-reduce.2.cloned.1.call-update) | async-done | bytes 81936 | tf_op jit(solution)/shard_map/psum | solution.py:248
  139.3 1.2 multiply_subtract_fusion.2
  140.5 1.1 multiply_subtract_fusion.1
  141.6 1.0 multiply_subtract_fusion.10
  142.6 1.1 multiply_subtract_fusion.3
  143.7 0.1 multiply_add_fusion.26
  143.8 16.4 %fusion.14 = f32[500,4,2,128]{3,2,1,0:T(2,128)S(1)} fusion(f32[4,2,128]{2,1,0:T(2,128)S(1)} %bitcast.102, f32[4,2,128]{2,1,0:T(2,128)S(1)} %bitcast.105, f32[4,2,128]{2,1,0:T(2,128)S(1)} %bitcast.104, f32[4,2,128]{2,1,0:T(2,128)S(1)} %bitcast.103, f32[4,2,128]{2,1,0:T(2,128)S(1)} %bitcast.106, f32[4,2,128]{2,1,0:T(2,128)S(1)} %bitcast.101, ...), kind=kLoop, calls=%fused_computation.41 | loop fusion | flops 25600000 | bytes 2135920 | tf_op jit(solution)/shard_map/mul | solution.py:192
  160.3 0.9 add_multiply_fusion
  161.2 0.0 collective-permute-done.2
  161.2 0.0 collective-permute-done.3
  161.2 4.0 %fusion.31 = (f32[500,2,128]{2,1,0:T(2,128)S(1)}, f32[500,2,128]{2,1,0:T(2,128)S(1)}, f32[500,2,128]{2,1,0:T(2,128)S(1)}, f32[500,2,128]{2,1,0:T(2,128)S(1)}) fusion(f32[500,3,1,128]{3,2,0,1:T(1,128)} %collective-permute-done.3, f32[500,3,1,128]{3,2,0,1:T(1,128)} %collective-permute-done.2, f32[500,3,2,128]{3,2,1,0:T(2,128)S(1)} %copy-done), kind=kLoop, calls=%fused_computation.66 | loop fusion | flops 1024000 | bytes 5120000 | tf_op jit(solution)/shard_map/squeeze | solution.py:258
  165.2 0.6 slice_bitcast_fusion.3
  165.8 0.0 copy-start.1
  165.8 0.0 copy-start.3
  165.8 1.4 fusion.40
  167.2 0.9 pad_maximum_fusion.6
  168.2 6.2 %multiply_add_fusion.5 = (f32[500,1,2,128]{3,2,1,0:T(2,128)S(1)}, f32[500,1,2,128]{3,2,1,0:T(2,128)S(1)}, f32[500,1,2,128]{3,2,1,0:T(2,128)S(1)}) fusion(f32[500]{0:T(512)S(1)} %get-tuple-element.122, f32[500]{0:T(512)S(1)} %broadcast_multiply_fusion.3, f32[500,1,2,128]{3,2,1,0:T(2,128)S(1)} %bitcast.76, f32[500,1,2,128]{3,2,1,0:T(2,128)S(1)} %copy-done.3, ...), kind=kLoop, calls=%fused_computation.88 | loop fusion | flops 2304000 | bytes 9221120 | tf_op jit(solution)/shard_map/add | solution.py:215
  174.4 4.7 %fusion.29 = f32[500,1,2,128]{3,2,1,0:T(2,128)S(1)} fusion(f32[500,3,2,128]{3,2,1,0:T(2,128)S(1)} %copy-done, f32[500,3,2,1]{3,2,1,0:T(2,128)S(1)} %copy-done.1, f32[500,3,2,1]{3,2,1,0:T(2,128)S(1)} %copy.18, pred[500]{0:T(512)(128)(4,1)S(1)} %get-tuple-element.6, f32[500]{0:T(512)S(1)} %broadcast_multiply_fusion, f32[500]{0:T(512)S(1)} %broadcast_multiply_fusion.3, ...), kind=kLoop, calls=%fused_computation.62 | loop fusion | flops 1792000 | bytes 8197120 | tf_op jit(solution)/shard_map/add | solution.py:219
  179.1 1.8 broadcast_select_fusion
  180.8 2.8 %multiply_add_fusion.4 = f32[500,1,2,128]{3,2,1,0:T(2,128)S(1)} fusion(f32[500,1,2,128]{3,2,1,0:T(2,128)S(1)} %bitcast.82, f32[500,1,2,128]{3,2,1,0:T(2,128)S(1)} %bitcast.81, f32[500,1,2,128]{3,2,1,0:T(2,128)S(1)} %get-tuple-element.53, f32[500,1,2,128]{3,2,1,0:T(2,128)S(1)} %get-tuple-element.52, pred[500]{0:T(512)(128)(4,1)S(1)} %get-tuple-element.5, ...), kind=kLoop, calls=%fused_computation.87 | loop fusion | flops 1024000 | bytes 3588500 | tf_op jit(solution)/shard_map/add | solution.py:216
  183.7 2.5 %maximum_add_fusion = f32[500,3,2,128]{3,2,1,0:T(2,128)} fusion(f32[500,1,2,128]{3,2,1,0:T(2,128)S(1)} %fusion.29, f32[500,1,2,128]{3,2,1,0:T(2,128)S(1)} %multiply_add_fusion.4, f32[500,1,2,128]{3,2,1,0:T(2,128)S(1)} %get-tuple-element.51, f32[500,3,2,128]{3,2,1,0:T(2,128)S(1)} %copy-done, f32[500,1,2,128]{3,2,1,0:T(2,128)S(1)} %get-tuple-element.64, ...), kind=kLoop, calls=%fused_computation.54 | loop fusion | flops 2688000 | bytes 6144000 | tf_op jit(solution)/shard_map/add | solution.py:288
  (37 shorter events, 0.3 us)
Async XLA Ops:
  6.5 132.8 %all-reduce.2.cloned.1.call-start = ((), (), s32[]{:S(2)}) async-start(), calls=%async_computation | async-start | bytes 196608 | tf_op jit(solution)/shard_map/psum | solution.py:248
  10.0 43.4 %copy-start.2 = (f32[500,1,2,128]{3,2,1,0:T(2,128)}, f32[500,1,2,128]{3,2,1,0:T(2,128)S(1)}, u32[]{:S(2)}) copy-start(f32[500,1,2,128]{3,2,1,0:T(2,128)S(1)} %get-tuple-element.73) | copy-start | bytes 1536004
  10.1 44.3 %copy-start.6 = (f32[500,1,2,128]{3,2,1,0:T(2,128)}, f32[500,1,2,128]{3,2,1,0:T(2,128)S(1)}, u32[]{:S(2)}) copy-start(f32[500,1,2,128]{3,2,1,0:T(2,128)S(1)} %get-tuple-element.74) | copy-start | bytes 1536004
  10.1 45.3 %copy-start.4 = (f32[500,1,2,128]{3,2,1,0:T(2,128)}, f32[500,1,2,128]{3,2,1,0:T(2,128)S(1)}, u32[]{:S(2)}) copy-start(f32[500,1,2,128]{3,2,1,0:T(2,128)S(1)} %get-tuple-element.75) | copy-start | bytes 1536004
  24.0 5.1 %copy-start = (f32[500,3,2,128]{3,2,1,0:T(2,128)S(1)}, f32[500,3,2,128]{3,2,1,0:T(2,128)}, u32[]{:S(2)}) copy-start(f32[500,3,2,128]{3,2,1,0:T(2,128)} %param.5) | copy-start | bytes 4608004
  31.4 129.7 %collective-permute-start.2 = (f32[500,3,1,128]{3,2,0,1:T(1,128)}, f32[500,3,1,128]{3,2,0,1:T(1,128)}, u32[]{:S(2)}, u32[]{:S(2)}) collective-permute-start(f32[500,3,1,128]{3,2,0,1:T(1,128)} %get-tuple-element.78), channel_id=1, source_target_pairs={{16,0},{17,1},{18,2},{19,3},{20,4},{21,5},{22,6},{23,7},{24,8},{25... | collective-permute-start | bytes 2304008 | tf_op jit(solution)/shard_map/ppermute | solution.py:26
  32.7 128.5 %collective-permute-start.3 = (f32[500,3,1,128]{3,2,0,1:T(1,128)}, f32[500,3,1,128]{3,2,0,1:T(1,128)}, u32[]{:S(2)}, u32[]{:S(2)}) collective-permute-start(f32[500,3,1,128]{3,2,0,1:T(1,128)} %get-tuple-element.79), channel_id=1, source_target_pairs={{0,16},{1,17},{2,18},{3,19},{4,20},{5,21},{6,22},{7,23},{8,24},{9,... | collective-permute-start | bytes 2304008 | tf_op jit(solution)/shard_map/ppermute | solution.py:23
  43.7 9.6 %copy-start.11 = (s32[500,2]{0,1:T(2,128)S(1)}, s32[500,2]{0,1:T(2,128)}, u32[]{:S(2)}) copy-start(s32[500,2]{0,1:T(2,128)} %param.6) | copy-start | bytes 12004
  43.7 9.6 %copy-start.12 = (s32[2,128]{1,0:T(2,128)S(1)}, s32[2,128]{1,0:T(2,128)}, u32[]{:S(2)}) copy-start(s32[2,128]{1,0:T(2,128)} %param.7) | copy-start | bytes 3076
  46.2 11.8 %collective-permute-start = (f32[500,3,2,1]{0,2,3,1:T(2,128)S(1)}, f32[500,3,2,1]{0,2,3,1:T(2,128)S(1)}, u32[]{:S(2)}, u32[]{:S(2)}) collective-permute-start(f32[500,3,2,1]{0,2,3,1:T(2,128)S(1)} %copy.33), channel_id=1, source_target_pairs={{32,0},{64,32},{96,64},{128,96},{160,128},{192,160},{224,192},{0,2... | collective-permute-start | bytes 36008 | tf_op jit(solution)/shard_map/ppermute | solution.py:26
  53.2 7.1 %collective-permute-start.1 = (f32[500,3,2,1]{0,2,3,1:T(2,128)S(1)}, f32[500,3,2,1]{0,2,3,1:T(2,128)S(1)}, u32[]{:S(2)}, u32[]{:S(2)}) collective-permute-start(f32[500,3,2,1]{0,2,3,1:T(2,128)S(1)} %copy.34), channel_id=1, source_target_pairs={{0,32},{32,64},{64,96},{96,128},{128,160},{160,192},{192,224},{224... | collective-permute-start | bytes 36008 | tf_op jit(solution)/shard_map/ppermute | solution.py:23
  161.1 4.1 %copy-start.10 = (f32[125,2,2,2,128]{4,3,2,1,0:T(2,128)S(1)}, f32[125,2,2,2,128]{4,3,2,1,0:T(2,128)}, u32[]{:S(2)}) copy-start(f32[125,2,2,2,128]{4,3,2,1,0:T(2,128)} %rev.10) | copy-start | bytes 1536004
  161.1 4.6 %copy-start.8 = (f32[125,2,2,2,128]{4,3,2,1,0:T(2,128)S(1)}, f32[125,2,2,2,128]{4,3,2,1,0:T(2,128)}, u32[]{:S(2)}) copy-start(f32[125,2,2,2,128]{4,3,2,1,0:T(2,128)} %rev.12) | copy-start | bytes 1536004
  161.1 4.6 %copy-start.9 = (f32[125,2,2,2,128]{4,3,2,1,0:T(2,128)S(1)}, f32[125,2,2,2,128]{4,3,2,1,0:T(2,128)}, u32[]{:S(2)}) copy-start(f32[125,2,2,2,128]{4,3,2,1,0:T(2,128)} %rev.11) | copy-start | bytes 1536004
  165.8 2.3 %copy-start.1 = (f32[500,3,2,1]{3,2,1,0:T(2,128)S(1)}, f32[500,3,2,1]{3,2,1,0:T(2,128)}, u32[]{:S(2)}) copy-start(f32[500,3,2,1]{3,2,1,0:T(2,128)} %copy.20) | copy-start | bytes 36004
  165.8 2.3 %copy-start.3 = (f32[500,1,2,128]{3,2,1,0:T(2,128)S(1)}, f32[500,1,2,128]{3,2,1,0:T(2,128)}, u32[]{:S(2)}) copy-start(f32[500,1,2,128]{3,2,1,0:T(2,128)} %copy-done.2) | copy-start | bytes 1536004
  165.8 2.3 %copy-start.5 = (f32[500,1,2,128]{3,2,1,0:T(2,128)S(1)}, f32[500,1,2,128]{3,2,1,0:T(2,128)}, u32[]{:S(2)}) copy-start(f32[500,1,2,128]{3,2,1,0:T(2,128)} %copy-done.4) | copy-start | bytes 1536004
  174.4 4.7 %copy-start.7 = (f32[500,1,2,128]{3,2,1,0:T(2,128)S(1)}, f32[500,1,2,128]{3,2,1,0:T(2,128)}, u32[]{:S(2)}) copy-start(f32[500,1,2,128]{3,2,1,0:T(2,128)} %copy-done.6) | copy-start | bytes 1536004
Sparse Core Ops, SparseCore 0:
  29.2 110.0 all-reduce.1
where the time goes:
time: 194 us; the launch traced here: 193 us
  waiting for transfers between devices  79.8 us (41%)
  other arithmetic  56.9 us (29%)
  local copies, waits for them, and re-layouts  25 us (13%)
  between operations  13.8 us (7%)
  starting transfers between devices  13.2 us (7%)
  matrix products  4.37 us (2%)
    psum x1, waiting for transfers between devices, shards(): params = gauss_params(lax.psum(partial_sums, 'vert'))  77 us
    mul x1, other arithmetic, gauss_tangent(): gauss * (params[10] + rel_x * params[11] + rel_y * params[12] + rel_z * p...  16.4 us
    ppermute x2, starting transfers between devices, padded(): lax.ppermute(lax.slice_in_dim(block, block.shape[dim] - width, None, axis...  7.33 us
    add x1, other arithmetic, transport(): speed_x * (right_val - left_val) + speed_y * (top_val - bottom_val)  6.21 us
    slice x2, local copies, waits for them, and re-layouts, padded(): lax.slice_in_dim(block, 0, width, axis=dim)  6.09 us
    ppermute x2, starting transfers between devices, padded(): lax.ppermute(lax.slice_in_dim(block, 0, width, axis=dim), axis, backward)  5.82 us
    unnamed x28, local copies, waits for them, and re-layouts  4.98 us
    add x2, other arithmetic, gauss_points(): center + XI_SIGNS[q] * GAUSS * grad_x + ETA_SIGNS[q] * GAUSS * grad_y  4.89 us
  transfers between devices with their start and end apart: 5, of which 3 were waited for; matrix products, arithmetic and copies ran while one was open for 20% of the time, Pallas kernels for 0%

commit v1 on v0

--- a/solution.py
+++ b/solution.py
@@ -245,7 +245,7 @@
     partial_sums = jnp.concatenate(
         [partial_sums[:, :point_count], partial_sums[:, point_count:]], axis=0
     )
-    params = gauss_params(lax.psum(partial_sums, "vert"))
+    params = gauss_params(jnp.sum(lax.all_gather(partial_sums, "vert"), axis=0))
     center, grad_x, grad_y = (tangent[:, 0], tangent[:, 1], tangent[:, 2])
     x_padded = padded(tangent, (("gx", 3),), 1, True)
     western = x_padded[:, :, :, :-2]

time: 194 us -> 118 us (0.61)
  waiting for transfers between devices: 79.8 us -> 2.79 us
    psum x1 -> x0, waiting for transfers between devices: 77 us -> none  [shards(): params = gauss_params(lax.psum(partial_sums, 'vert'))]
    sub x2, other arithmetic: 2.27 us -> 0.1 us  [gauss_params(): moments[14 + duo_ordinal] / density]
    unnamed x28 -> x34, local copies, waits for them, and re-layouts: 4.98 us -> 5.48 us
  transfers between devices with their start and end apart: 5 -> 5, of which waited for: 3 -> 2; matrix products, arithmetic and copies ran while one was open for 20% -> 36% of each run, Pallas kernels for 0% -> 0%
where the time goes in v1:
time: 118 us; the launch traced here: 116 us
  other arithmetic  56.9 us (48%)
  local copies, waits for them, and re-layouts  25.5 us (22%)
  between operations  13.8 us (12%)
  starting transfers between devices  13.1 us (11%)
  matrix products  4.37 us (4%)
  waiting for transfers between devices  2.79 us (2%)
    mul x1, other arithmetic, gauss_tangent(): gauss * (params[10] + rel_x * params[11] + rel_y * params[12] + rel_z * p...  16.4 us
    ppermute x2, starting transfers between devices, padded(): lax.ppermute(lax.slice_in_dim(block, block.shape[dim] - width, None, axis...  7.34 us
    add x1, other arithmetic, transport(): speed_x * (right_val - left_val) + speed_y * (top_val - bottom_val)  6.84 us
    slice x2, local copies, waits for them, and re-layouts, padded(): lax.slice_in_dim(block, 0, width, axis=dim)  6.07 us
    add x1, other arithmetic, transport(): speed_x * (right_slope - left_slope)  5.84 us
    ppermute x2, starting transfers between devices, padded(): lax.ppermute(lax.slice_in_dim(block, 0, width, axis=dim), axis, backward)  5.78 us
    unnamed x34, local copies, waits for them, and re-layouts  5.48 us
    add x2, other arithmetic, gauss_points(): center + XI_SIGNS[q] * GAUSS * grad_x + ETA_SIGNS[q] * GAUSS * grad_y  4.89 us
  transfers between devices with their start and end apart: 5, of which 2 were waited for; matrix products, arithmetic and copies ran while one was open for 36% of the time, Pallas kernels for 0%

profile of v1, /device:TPU:1, one launch (start us, length us, event | category | flops | bytes accessed | tf_op | source)
XLA Modules:
  0.0 116.5 jit_solution(10327730085306393507)
XLA Ops:
  6.5 0.8 fusion.80
  7.5 2.6 %multiply_add_fusion.9 = (f32[500,1,2,128]{3,2,1,0:T(2,128)S(1)}, f32[500,1,2,128]{3,2,1,0:T(2,128)S(1)}, f32[500,1,2,128]{3,2,1,0:T(2,128)S(1)}, f32[500,1,2,12...) fusion(f32[500,3,2,128]{3,2,1,0:T(2,128)} %param.5), kind=kLoop, calls=%fused_computation.98 | loop fusion | flops 1536000 | bytes 5120000 | tf_op jit(solution)/shard_map/add | solution.py:64
  10.1 1.9 %pad_maximum_fusion.1 = f32[500,4,2,128]{3,2,1,0:T(2,128)} fusion(f32[500,1,2,128]{3,2,1,0:T(2,128)S(1)} %get-tuple-element.71, f32[500,1,2,128]{3,2,1,0:T(2,128)S(1)} %get-tuple-element.72, f32[500,1,2,128]{3,2,1,0:T(2,128)S(1)} %get-tuple-element.70, f32[500,1,2,128]{3,2,1,0:T(2,128)S(1)} %get-tuple-element.69), kind=kLoop, calls=%fused_computation.53 | loop fusion | flops 1536000 | bytes 4096000 | tf_op jit(solution)/shard_map/stack | solution.py:63
  12.0 3.9 %reshape.660 = f32[500,1024]{1,0:T(8,128)} reshape(f32[500,4,2,128]{3,2,1,0:T(2,128)} %pad_maximum_fusion.1) | data formatting | bytes 4096000 | tf_op jit(solution)/shard_map/reshape | solution.py:238
  15.9 2.3 %multiply_add_fusion.13 = (f32[500,1,2,128]{3,2,1,0:T(2,128)S(1)}, f32[500,1,2,128]{3,2,1,0:T(2,128)S(1)}, f32[500,1,2,128]{3,2,1,0:T(2,128)S(1)}, f32[500,1,2,128]{3,2,1,0:T(2,128)S(1)}) fusion(f32[500,3,2,128]{3,2,1,0:T(2,128)} %param.4), kind=kLoop, calls=%fused_computation.102 | loop fusion | flops 1280000 | bytes 3584000 | tf_op jit(solution)/shard_map/add | solution.py:64
  18.2 1.9 %pad_maximum_fusion = f32[500,4,2,128]{3,2,1,0:T(2,128)} fusion(f32[500,1,2,128]{3,2,1,0:T(2,128)S(1)} %get-tuple-element.67, f32[500,1,2,128]{3,2,1,0:T(2,128)S(1)} %get-tuple-element.66, f32[500,1,2,128]{3,2,1,0:T(2,128)S(1)} %get-tuple-element.68, f32[500,1,2,128]{3,2,1,0:T(2,128)S(1)} %get-tuple-element.65), kind=kLoop, calls=%fused_computation.52 | loop fusion | flops 1536000 | bytes 4096000 | tf_op jit(solution)/shard_map/stack | solution.py:63
  20.1 3.9 %reshape.659 = f32[500,1024]{1,0:T(8,128)} reshape(f32[500,4,2,128]{3,2,1,0:T(2,128)} %pad_maximum_fusion) | data formatting | bytes 4096000 | tf_op jit(solution)/shard_map/reshape | solution.py:237
  24.0 0.1 stack.11
  24.1 4.4 %fusion = f32[10,2048]{1,0:T(8,128)S(1)} fusion(f32[500,1024]{1,0:T(8,128)} %reshape.660, f32[500,1024]{1,0:T(8,128)} %reshape.659, f32[10,500]{1,0:T(8,128)S(1)} %stack.11), kind=kOutput, calls=%fused_computation.27 | convolution fusion | flops 123909000 | bytes 4197920 | tf_op jit(solution)/shard_map/dot_general | solution.py:242
  28.5 0.7 maximum_bitcast_fusion
  29.1 0.0 all-gather.4.cloned.1.call-update
  29.2 2.3 %fusion.102 = (f32[500,3,1,128]{3,2,0,1:T(1,128)}, f32[500,3,1,128]{3,2,0,1:T(1,128)}) fusion(f32[500,3,2,128]{3,2,1,0:T(2,128)S(1)} %copy-done), kind=kLoop, calls=%fused_computation.265 | loop fusion | bytes 3072000 | tf_op jit(solution)/shard_map/slice | solution.py:26
  31.5 1.3 %collective-permute-start.2 = (f32[500,3,1,128]{3,2,0,1:T(1,128)}, f32[500,3,1,128]{3,2,0,1:T(1,128)}, u32[]{:S(2)}, u32[]{:S(2)}) collective-permute-start(f32[500,3,1,128]{3,2,0,1:T(1,128)} %get-tuple-element.78), channel_id=1, source_target_pairs={{16,0},{17,1},{18,2},{19,3},{20,4},{21,5},{22,6},{23,7},{24,8},{25... | collective-permute-start | bytes 2304008 | tf_op jit(solution)/shard_map/ppermute | solution.py:26
  32.8 7.3 %collective-permute-start.3 = (f32[500,3,1,128]{3,2,0,1:T(1,128)}, f32[500,3,1,128]{3,2,0,1:T(1,128)}, u32[]{:S(2)}, u32[]{:S(2)}) collective-permute-start(f32[500,3,1,128]{3,2,0,1:T(1,128)} %get-tuple-element.79), channel_id=1, source_target_pairs={{0,16},{1,17},{2,18},{3,19},{4,20},{5,21},{6,22},{7,23},{8,24},{9,... | collective-permute-start | bytes 2304008 | tf_op jit(solution)/shard_map/ppermute | solution.py:23
  40.0 3.8 %fusion.103 = (f32[500,3,2,1]{3,2,1,0:T(2,128)}, f32[500,3,2,1]{3,2,1,0:T(2,128)}) fusion(f32[500,3,2,128]{3,2,1,0:T(2,128)S(1)} %copy-done), kind=kLoop, calls=%fused_computation.266 | loop fusion | bytes 48000 | tf_op jit(solution)/shard_map/slice | solution.py:26
  43.8 2.5 %copy.33 = f32[500,3,2,1]{0,2,3,1:T(2,128)S(1)} copy(f32[500,3,2,1]{3,2,1,0:T(2,128)} %get-tuple-element.80) | data formatting | bytes 24000
  46.3 4.5 %collective-permute-start = (f32[500,3,2,1]{0,2,3,1:T(2,128)S(1)}, f32[500,3,2,1]{0,2,3,1:T(2,128)S(1)}, u32[]{:S(2)}, u32[]{:S(2)}) collective-permute-start(f32[500,3,2,1]{0,2,3,1:T(2,128)S(1)} %copy.33), channel_id=1, source_target_pairs={{32,0},{64,32},{96,64},{128,96},{160,128},{192,160},{224,192},{0,2... | collective-permute-start | bytes 36008 | tf_op jit(solution)/shard_map/ppermute | solution.py:26
  50.8 2.5 %copy.34 = f32[500,3,2,1]{0,2,3,1:T(2,128)S(1)} copy(f32[500,3,2,1]{3,2,1,0:T(2,128)} %get-tuple-element.81) | data formatting | bytes 24000
  53.3 0.1 collective-permute-start.1
  53.5 1.0 rev.11
  54.5 1.0 rev.12
  55.5 1.0 rev.10
  56.5 1.1 collective-permute-done
  57.6 1.1 copy.18
  58.7 1.6 %collective-permute-done.1 = f32[500,3,2,1]{0,2,3,1:T(2,128)S(1)} collective-permute-done((f32[500,3,2,1]{0,2,3,1:T(2,128)S(1)}, f32[500,3,2,1]{0,2,3,1:T(2,128)S(1)}, u32[]{:S(2)}, u32[]{:S(2)}) %collective-permute-start.1) | collective-permute-done | bytes 12032 | tf_op jit(solution)/shard_map/ppermute | solution.py:23
  60.3 2.0 %copy.20 = f32[500,3,2,1]{3,2,1,0:T(2,128)} copy(f32[500,3,2,1]{0,2,3,1:T(2,128)S(1)} %collective-permute-done.1) | data formatting | bytes 24000 | tf_op jit(solution)/shard_map/ppermute | solution.py:23
  62.4 0.0 collective-permute-done.2
  62.4 4.0 %fusion.31 = (f32[500,2,128]{2,1,0:T(2,128)S(1)}, f32[500,2,128]{2,1,0:T(2,128)S(1)}, f32[500,2,128]{2,1,0:T(2,128)S(1)}, f32[500,2,128]{2,1,0:T(2,128)S(1)}) fusion(f32[500,3,1,128]{3,2,0,1:T(1,128)} %collective-permute-done.3, f32[500,3,1,128]{3,2,0,1:T(1,128)} %collective-permute-done.2, f32[500,3,2,128]{3,2,1,0:T(2,128)S(1)} %copy-done), kind=kLoop, calls=%fused_computation.66 | loop fusion | flops 1024000 | bytes 5120000 | tf_op jit(solution)/shard_map/squeeze | solution.py:258
  66.4 1.4 %fusion.40 = (f32[500,1,1,128]{3,1,2,0:T(1,128)S(1)}, f32[500,1,1,128]{3,1,2,0:T(1,128)S(1)}, f32[500,1,1,128]{3,1,2,0:T(1,128)S(1)}, f32[500,1,1,128]{3,1,2,0:T...) fusion(pred[]{:T(512)S(6)} %eq.34, f32[500,2,128]{2,1,0:T(2,128)S(1)} %get-tuple-element.58, ...), kind=kLoop, calls=%fused_computation.106 | loop fusion | flops 384000 | bytes 3841026 | tf_op jit(solution)/shard_map/concatenate | solution.py:268
  67.8 0.0 copy-start.1
  67.9 0.9 pad_maximum_fusion.6
  68.8 1.8 %broadcast_select_fusion = f32[500,1,2,128]{3,1,2,0:T(1,128)S(1)} fusion(f32[500,1,2,128]{3,1,2,0:T(1,128)S(1)} %bitcast.81, pred[500]{0:T(512)(128)(4,1)S(1)} %get-tuple-element.5, f32[500,1,1,128]{3,1,2,0:T(1,128)S(1)} %get-tuple-element.83, f32[500,1,1,128]{3,1,2,0:T(1,128)S(1)} %get-tuple-element.84), kind=kLoop, calls=%fused_computation.57 | loop fusion | flops 256000 | bytes 1536500 | tf_op jit(solution)/shard_map/jit(_where)/select_n | solution.py:210
  70.6 0.6 slice_bitcast_fusion.3
  71.1 6.8 %multiply_add_fusion.5 = (f32[500,1,2,128]{3,2,1,0:T(2,128)}, f32[500,1,2,128]{3,2,1,0:T(2,128)S(1)}, f32[500,1,2,128]{3,2,1,0:T(2,128)S(1)}) fusion(f32[500]{0:T(512)S(1)} %get-tuple-element.122, f32[500]{0:T(512)S(1)} %broadcast_multiply_fusion.3, f32[500,1,2,128]{3,2,1,0:T(2,128)S(1)} %bitcast.78, f32[500,1,2,128]{3,2,1,0:T(2,128)S(1)} %copy-done.3, ...), kind=kLoop, calls=%fused_computation.88 | loop fusion | flops 2304000 | bytes 9221120 | tf_op jit(solution)/shard_map/add | solution.py:215
  78.0 3.6 %multiply_add_fusion.4 = f32[500,1,2,128]{3,2,1,0:T(2,128)} fusion(f32[500,1,2,128]{3,2,1,0:T(2,128)S(1)} %bitcast.84, f32[500,1,2,128]{3,2,1,0:T(2,128)S(1)} %bitcast.83, f32[500,1,2,128]{3,2,1,0:T(2,128)S(1)} %get-tuple-element.53, f32[500,1,2,128]{3,2,1,0:T(2,128)S(1)} %get-tuple-element.52, pred[500]{0:T(512)(128)(4,1)S(1)} %get-tuple-element.5, ...), kind=kLoop, calls=%fused_computation.87 | loop fusion | flops 1024000 | bytes 3588500 | tf_op jit(solution)/shard_map/add | solution.py:216
  81.6 5.8 %fusion.29 = f32[500,1,2,128]{3,2,1,0:T(2,128)} fusion(f32[500,3,2,128]{3,2,1,0:T(2,128)S(1)} %copy-done, f32[500,3,2,1]{3,2,1,0:T(2,128)S(1)} %copy-done.1, f32[500,3,2,1]{3,2,1,0:T(2,128)S(1)} %copy.18, pred[500]{0:T(512)(128)(4,1)S(1)} %get-tuple-element.6, f32[500]{0:T(512)S(1)} %broadcast_multiply_fusion, f32[500]{0:T(512)S(1)} %broadcast_multiply_fusion.3, ...), kind=kLoop, calls=%fused_computation.62 | loop fusion | flops 1792000 | bytes 8197120 | tf_op jit(solution)/shard_map/add | solution.py:219
  87.4 1.5 %reduce_sum.9 = f32[20,1024]{1,0:T(8,128)S(1)} reduce(f32[16,20,1024]{2,1,0:T(8,128)} %all-gather.4.cloned.1.call-done, f32[]{:T(128)} %constant.94.clone.1), dimensions={0}, to_apply=%region_0.1 | reduce | flops 307200 | bytes 1392644 | tf_op jit(solution)/shard_map/reduce_sum | solution.py:248
  88.9 0.1 multiply_subtract_fusion.2
  89.0 0.1 multiply_subtract_fusion.10
  89.1 0.1 multiply_subtract_fusion.3
  89.3 0.1 multiply_add_fusion.26
  89.4 16.4 %fusion.14 = f32[500,4,2,128]{3,2,1,0:T(2,128)S(1)} fusion(f32[4,2,128]{2,1,0:T(2,128)S(1)} %bitcast.104, f32[4,2,128]{2,1,0:T(2,128)S(1)} %bitcast.107, f32[4,2,128]{2,1,0:T(2,128)S(1)} %bitcast.106, f32[4,2,128]{2,1,0:T(2,128)S(1)} %bitcast.105, f32[4,2,128]{2,1,0:T(2,128)S(1)} %bitcast.108, f32[4,2,128]{2,1,0:T(2,128)S(1)} %bitcast.103, ...), kind=kLoop, calls=%fused_computation.41 | loop fusion | flops 25600000 | bytes 2135920 | tf_op jit(solution)/shard_map/mul | solution.py:192
  105.9 0.0 copy-start.9
  105.9 0.9 add_multiply_fusion
  106.7 0.1 copy-done.8
  106.9 0.2 copy-done.9
  107.0 0.2 copy-done.10
  107.2 2.4 %maximum_add_fusion = f32[500,3,2,128]{3,2,1,0:T(2,128)} fusion(f32[500,1,2,128]{3,2,1,0:T(2,128)S(1)} %copy-done.9, f32[500,1,2,128]{3,2,1,0:T(2,128)S(1)} %copy-done.10, f32[500,1,2,128]{3,2,1,0:T(2,128)S(1)} %copy-done.8, f32[500,3,2,128]{3,2,1,0:T(2,128)S(1)} %copy-done, f32[500,1,2,128]{3,2,1,0:T(2,128)S(1)} %get-tuple-element.64, ...), kind=kLoop, calls=%fused_computation.54 | loop fusion | flops 2688000 | bytes 6144000 | tf_op jit(solution)/shard_map/add | solution.py:288
  (44 shorter events, 0.4 us)
Async XLA Ops:
  6.5 80.9 %all-gather.4.cloned.1.call-start = ((), (), s32[]{:S(2)}) async-start(), calls=%async_computation | async-start | bytes 1671168 | tf_op jit(solution)/shard_map/all_gather | solution.py:248
  10.0 43.4 %copy-start.2 = (f32[500,1,2,128]{3,2,1,0:T(2,128)}, f32[500,1,2,128]{3,2,1,0:T(2,128)S(1)}, u32[]{:S(2)}) copy-start(f32[500,1,2,128]{3,2,1,0:T(2,128)S(1)} %get-tuple-element.73) | copy-start | bytes 1536004
  10.1 44.4 %copy-start.6 = (f32[500,1,2,128]{3,2,1,0:T(2,128)}, f32[500,1,2,128]{3,2,1,0:T(2,128)S(1)}, u32[]{:S(2)}) copy-start(f32[500,1,2,128]{3,2,1,0:T(2,128)S(1)} %get-tuple-element.74) | copy-start | bytes 1536004
  10.1 45.4 %copy-start.4 = (f32[500,1,2,128]{3,2,1,0:T(2,128)}, f32[500,1,2,128]{3,2,1,0:T(2,128)S(1)}, u32[]{:S(2)}) copy-start(f32[500,1,2,128]{3,2,1,0:T(2,128)S(1)} %get-tuple-element.75) | copy-start | bytes 1536004
  24.1 5.1 %copy-start = (f32[500,3,2,128]{3,2,1,0:T(2,128)S(1)}, f32[500,3,2,128]{3,2,1,0:T(2,128)}, u32[]{:S(2)}) copy-start(f32[500,3,2,128]{3,2,1,0:T(2,128)} %param.5) | copy-start | bytes 4608004
  31.5 30.9 %collective-permute-start.2 = (f32[500,3,1,128]{3,2,0,1:T(1,128)}, f32[500,3,1,128]{3,2,0,1:T(1,128)}, u32[]{:S(2)}, u32[]{:S(2)}) collective-permute-start(f32[500,3,1,128]{3,2,0,1:T(1,128)} %get-tuple-element.78), channel_id=1, source_target_pairs={{16,0},{17,1},{18,2},{19,3},{20,4},{21,5},{22,6},{23,7},{24,8},{25... | collective-permute-start | bytes 2304008 | tf_op jit(solution)/shard_map/ppermute | solution.py:26
  32.8 29.6 %collective-permute-start.3 = (f32[500,3,1,128]{3,2,0,1:T(1,128)}, f32[500,3,1,128]{3,2,0,1:T(1,128)}, u32[]{:S(2)}, u32[]{:S(2)}) collective-permute-start(f32[500,3,1,128]{3,2,0,1:T(1,128)} %get-tuple-element.79), channel_id=1, source_target_pairs={{0,16},{1,17},{2,18},{3,19},{4,20},{5,21},{6,22},{7,23},{8,24},{9,... | collective-permute-start | bytes 2304008 | tf_op jit(solution)/shard_map/ppermute | solution.py:23
  43.8 9.6 %copy-start.14 = (s32[500,2]{0,1:T(2,128)S(1)}, s32[500,2]{0,1:T(2,128)}, u32[]{:S(2)}) copy-start(s32[500,2]{0,1:T(2,128)} %param.6) | copy-start | bytes 12004
  43.8 9.6 %copy-start.15 = (s32[2,128]{1,0:T(2,128)S(1)}, s32[2,128]{1,0:T(2,128)}, u32[]{:S(2)}) copy-start(s32[2,128]{1,0:T(2,128)} %param.7) | copy-start | bytes 3076
  46.3 11.3 %collective-permute-start = (f32[500,3,2,1]{0,2,3,1:T(2,128)S(1)}, f32[500,3,2,1]{0,2,3,1:T(2,128)S(1)}, u32[]{:S(2)}, u32[]{:S(2)}) collective-permute-start(f32[500,3,2,1]{0,2,3,1:T(2,128)S(1)} %copy.33), channel_id=1, source_target_pairs={{32,0},{64,32},{96,64},{128,96},{160,128},{192,160},{224,192},{0,2... | collective-permute-start | bytes 36008 | tf_op jit(solution)/shard_map/ppermute | solution.py:26
  53.3 7.1 %collective-permute-start.1 = (f32[500,3,2,1]{0,2,3,1:T(2,128)S(1)}, f32[500,3,2,1]{0,2,3,1:T(2,128)S(1)}, u32[]{:S(2)}, u32[]{:S(2)}) collective-permute-start(f32[500,3,2,1]{0,2,3,1:T(2,128)S(1)} %copy.34), channel_id=1, source_target_pairs={{0,32},{32,64},{64,96},{96,128},{128,160},{160,192},{192,224},{224... | collective-permute-start | bytes 36008 | tf_op jit(solution)/shard_map/ppermute | solution.py:23
  62.4 4.0 %copy-start.11 = (f32[125,2,2,2,128]{4,3,2,1,0:T(2,128)S(1)}, f32[125,2,2,2,128]{4,3,2,1,0:T(2,128)}, u32[]{:S(2)}) copy-start(f32[125,2,2,2,128]{4,3,2,1,0:T(2,128)} %rev.12) | copy-start | bytes 1536004
  62.4 4.0 %copy-start.12 = (f32[125,2,2,2,128]{4,3,2,1,0:T(2,128)S(1)}, f32[125,2,2,2,128]{4,3,2,1,0:T(2,128)}, u32[]{:S(2)}) copy-start(f32[125,2,2,2,128]{4,3,2,1,0:T(2,128)} %rev.11) | copy-start | bytes 1536004
  66.4 2.4 %copy-start.7 = (f32[500,1,2,128]{3,2,1,0:T(2,128)S(1)}, f32[500,1,2,128]{3,2,1,0:T(2,128)}, u32[]{:S(2)}) copy-start(f32[500,1,2,128]{3,2,1,0:T(2,128)} %copy-done.6) | copy-start | bytes 1536004
  67.8 2.7 %copy-start.13 = (f32[125,2,2,2,128]{4,3,2,1,0:T(2,128)S(1)}, f32[125,2,2,2,128]{4,3,2,1,0:T(2,128)}, u32[]{:S(2)}) copy-start(f32[125,2,2,2,128]{4,3,2,1,0:T(2,128)} %rev.10) | copy-start | bytes 1536004
  67.8 3.3 %copy-start.1 = (f32[500,3,2,1]{3,2,1,0:T(2,128)S(1)}, f32[500,3,2,1]{3,2,1,0:T(2,128)}, u32[]{:S(2)}) copy-start(f32[500,3,2,1]{3,2,1,0:T(2,128)} %copy.20) | copy-start | bytes 36004
  67.8 3.3 %copy-start.3 = (f32[500,1,2,128]{3,2,1,0:T(2,128)S(1)}, f32[500,1,2,128]{3,2,1,0:T(2,128)}, u32[]{:S(2)}) copy-start(f32[500,1,2,128]{3,2,1,0:T(2,128)} %copy-done.2) | copy-start | bytes 1536004
  67.8 3.3 %copy-start.5 = (f32[500,1,2,128]{3,2,1,0:T(2,128)S(1)}, f32[500,1,2,128]{3,2,1,0:T(2,128)}, u32[]{:S(2)}) copy-start(f32[500,1,2,128]{3,2,1,0:T(2,128)} %copy-done.4) | copy-start | bytes 1536004
  105.8 1.0 copy-start.8
  105.9 1.2 %copy-start.9 = (f32[500,1,2,128]{3,2,1,0:T(2,128)S(1)}, f32[500,1,2,128]{3,2,1,0:T(2,128)}, u32[]{:S(2)}) copy-start(f32[500,1,2,128]{3,2,1,0:T(2,128)} %fusion.29) | copy-start | bytes 1536004
  105.9 1.3 %copy-start.10 = (f32[500,1,2,128]{3,2,1,0:T(2,128)S(1)}, f32[500,1,2,128]{3,2,1,0:T(2,128)}, u32[]{:S(2)}) copy-start(f32[500,1,2,128]{3,2,1,0:T(2,128)} %multiply_add_fusion.4) | copy-start | bytes 1536004
Sparse Core Ops, SparseCore 0:
  29.3 43.0 all-gather.3
